TPU v7x, 32 devices: a whole 2x2x4 slice. The times are simulated.
32 devices in a mesh: row: 4 (over x, core), col: 8 (over z, y).
Axes of the slice: x: 2, y: 2, z: 4, core: 2. Of those that a mesh axis runs over, the one named last changes fastest.
Arguments:
- optical_field: float32 [2, 512, 4096], P(None, 'row', 'col'), may hold values from -6 to 6
- index_panels: bfloat16 [5, 512, 4096], P(None, ('row', 'col')), may hold values from -4 to 4
Outputs:
- propagated: float32 [2, 512, 4096], P(None, 'row', 'col')
All inputs are finite; a program needn't handle non-finite values.
Results may differ from a plain program's by a relative error of at most 0.0003.
Values may be sent and summed in bfloat16 or wider, within the bound.
A program may use at most 64 MiB of HBM per device.

v0:
```python
import jax
import jax.numpy as jnp
from jax import lax
from jax.sharding import PartitionSpec as P

STEPS = 2
diffraction = 0.15
phase_gain = 0.25


def with_halo(cells, sides, width):
    for axis, dim in sides:
        count = lax.axis_size(axis)
        head = lax.slice_in_dim(cells, 0, width, axis=dim)
        tail = lax.slice_in_dim(cells, cells.shape[dim] - width, cells.shape[dim], axis=dim)
        cells = jnp.concatenate(
            [
                lax.ppermute(tail, axis, [(i, (i + 1) % count) for i in range(count)]),
                cells,
                lax.ppermute(head, axis, [((i + 1) % count, i) for i in range(count)]),
            ],
            axis=dim,
        )
    return cells


def laplace(padded):
    centre = padded[:, 2:-2, 2:-2]
    along_y = 16.0 * (padded[:, 1:-3, 2:-2] + padded[:, 3:-1, 2:-2]) - (
        padded[:, :-4, 2:-2] + padded[:, 4:, 2:-2]
    )
    along_x = 16.0 * (padded[:, 2:-2, 1:-3] + padded[:, 2:-2, 3:-1]) - (
        padded[:, 2:-2, :-4] + padded[:, 2:-2, 4:]
    )
    return (along_y + along_x - 60.0 * centre) / 12.0


def slope(padded, plane):
    centre = padded[:, 2:-2, 2:-2]
    total = diffraction * laplace(padded) + phase_gain * plane.astype(jnp.float32) * centre
    return jnp.stack([-total[1], total[0]])


def section_slope(state, plane):
    padded = with_halo(state, (("row", 1), ("col", 2)), 2)
    return slope(padded, plane)


def local(optical_field, index_panels):
    planes_all = lax.all_to_all(index_panels, "col", split_axis=2, concat_axis=1, tiled=True)
    field = optical_field
    planes = None
    for step_index in range(STEPS):
        first = 2 * step_index
        planes = planes_all[first : first + 3]
        first_slope = section_slope(field, planes[0])
        second_slope = section_slope(field + 0.5 * first_slope, planes[1])
        third_slope = section_slope(field + 0.5 * second_slope, planes[1])
        fourth_slope = section_slope(field + third_slope, planes[2])
        field = field + (first_slope + 2.0 * second_slope + 2.0 * third_slope + fourth_slope) / 6.0
    return field


def solution(mesh):
    in_specs = (P(None, "row", "col"), P(None, ("row", "col"), None))
    out_specs = P(None, "row", "col")
    return jax.shard_map(local, mesh=mesh, in_specs=in_specs, out_specs=out_specs, check_vma=False)
```

profile of v0, /device:TPU:0, one launch (start us, length us, event | category | flops | bytes accessed | tf_op | source)
XLA Modules:
  0.0 162.4 jit_solution(11394870547222477419)
XLA Ops:
  0.0 8.1 %copy.10 = bf16[5,16,4096]{1,0,2:T(8,128)(2,1)} copy(bf16[5,16,4096]{2,1,0:T(8,128)(2,1)} %param.3) | data formatting | bytes 1310720 | tf_op args[1]
  8.1 9.1 %reshape.60 = bf16[8,2,20480]{2,1,0:T(2,128)(2,1)} reshape(bf16[4096,5,16]{2,1,0:T(8,128)(2,1)} %bitcast.10) | data formatting | bytes 1310720
  17.2 7.3 %all-to-all-start = ((bf16[8,2,20480]{2,1,0:T(2,128)(2,1)}), bf16[8,2,20480]{2,1,0:T(2,128)(2,1)S(1)}, u32[]{:S(2)}, u32[]{:S(2)}) async-start(bf16[8,2,20480]{2,1,0:T(2,128)(2,1)} %reshape.60), calls=%async_computation | async-start | bytes 1310720 | tf_op jit(solution)/shard_map/all_to_all | solution.py:50
  27.8 2.1 %collective-permute-start.2 = (f32[2,132,2]{2,1,0:T(8,128)S(1)}, f32[2,132,2]{2,1,0:T(8,128)S(1)}, u32[]{:S(2)}, u32[]{:S(2)}) collective-permute-start(f32[2,132,2]{2,1,0:T(8,128)S(1)} %get-tuple-element.40), channel_id=1, source_target_pairs={{0,1},{1,2},{2,3},{3,4},{4,5},{5,6},{6,7},{7,0},{8,9},{9,10},{10,1... | collective-permute-start | bytes 6344 | tf_op jit(solution)/shard_map/ppermute | solution.py:18
  29.8 2.8 %collective-permute-start.3 = (f32[2,132,2]{2,1,0:T(8,128)S(1)}, f32[2,132,2]{2,1,0:T(8,128)S(1)}, u32[]{:S(2)}, u32[]{:S(2)}) collective-permute-start(f32[2,132,2]{2,1,0:T(8,128)S(1)} %get-tuple-element.41), channel_id=1, source_target_pairs={{1,0},{2,1},{3,2},{4,3},{5,4},{6,5},{7,6},{0,7},{9,8},{10,9},{11,1... | collective-permute-start | bytes 6344 | tf_op jit(solution)/shard_map/ppermute | solution.py:20
  32.6 10.5 %collective-permute-done.2 = f32[2,132,2]{2,1,0:T(8,128)S(1)} collective-permute-done((f32[2,132,2]{2,1,0:T(8,128)S(1)}, f32[2,132,2]{2,1,0:T(8,128)S(1)}, u32[]{:S(2)}, u32[]{:S(2)}) %collective-permute-start.2) | collective-permute-done | bytes 2144 | tf_op jit(solution)/shard_map/ppermute | solution.py:18
  43.4 7.3 %reshape.61 = bf16[4096,5,16]{2,1,0:T(8,128)(2,1)} reshape(bf16[8,2,20480]{2,1,0:T(2,128)(2,1)S(1)} %all-to-all-done) | data formatting | bytes 1310720
  50.7 6.4 %copy.17 = bf16[5,16,8,512]{3,2,1,0:T(8,128)(2,1)S(1)} copy(bf16[5,16,8,512]{1,0,3,2:T(8,128)(2,1)} %bitcast.9) | data formatting | bytes 1310720 | tf_op jit(solution)/shard_map/all_to_all | solution.py:50
  61.5 2.8 %collective-permute-start.6 = (f32[2,132,2]{2,1,0:T(8,128)S(1)}, f32[2,132,2]{2,1,0:T(8,128)S(1)}, u32[]{:S(2)}, u32[]{:S(2)}) collective-permute-start(f32[2,132,2]{2,1,0:T(8,128)S(1)} %get-tuple-element.36), channel_id=1, source_target_pairs={{0,1},{1,2},{2,3},{3,4},{4,5},{5,6},{6,7},{7,0},{8,9},{9,10},{10,1... | collective-permute-start | bytes 6344 | tf_op jit(solution)/shard_map/ppermute | solution.py:18
  64.3 2.0 %collective-permute-start.7 = (f32[2,132,2]{2,1,0:T(8,128)S(1)}, f32[2,132,2]{2,1,0:T(8,128)S(1)}, u32[]{:S(2)}, u32[]{:S(2)}) collective-permute-start(f32[2,132,2]{2,1,0:T(8,128)S(1)} %get-tuple-element.37), channel_id=1, source_target_pairs={{1,0},{2,1},{3,2},{4,3},{5,4},{6,5},{7,6},{0,7},{9,8},{10,9},{11,1... | collective-permute-start | bytes 6344 | tf_op jit(solution)/shard_map/ppermute | solution.py:20
  66.5 4.4 %collective-permute-done.6 = f32[2,132,2]{2,1,0:T(8,128)S(1)} collective-permute-done((f32[2,132,2]{2,1,0:T(8,128)S(1)}, f32[2,132,2]{2,1,0:T(8,128)S(1)}, u32[]{:S(2)}, u32[]{:S(2)}) %collective-permute-start.6) | collective-permute-done | bytes 2144 | tf_op jit(solution)/shard_map/ppermute | solution.py:18
  70.8 2.9 %collective-permute-done.7 = f32[2,132,2]{2,1,0:T(8,128)S(1)} collective-permute-done((f32[2,132,2]{2,1,0:T(8,128)S(1)}, f32[2,132,2]{2,1,0:T(8,128)S(1)}, u32[]{:S(2)}, u32[]{:S(2)}) %collective-permute-start.7) | collective-permute-done | bytes 2144 | tf_op jit(solution)/shard_map/ppermute | solution.py:20
  78.2 4.7 %collective-permute-start.11 = (f32[2,132,2]{2,1,0:T(8,128)S(1)}, f32[2,132,2]{2,1,0:T(8,128)S(1)}, u32[]{:S(2)}, u32[]{:S(2)}) collective-permute-start(f32[2,132,2]{2,1,0:T(8,128)S(1)} %get-tuple-element.33), channel_id=1, source_target_pairs={{1,0},{2,1},{3,2},{4,3},{5,4},{6,5},{7,6},{0,7},{9,8},{10,9},{11,1... | collective-permute-start | bytes 6344 | tf_op jit(solution)/shard_map/ppermute | solution.py:20
  82.9 4.6 %collective-permute-done.10 = f32[2,132,2]{2,1,0:T(8,128)S(1)} collective-permute-done((f32[2,132,2]{2,1,0:T(8,128)S(1)}, f32[2,132,2]{2,1,0:T(8,128)S(1)}, u32[]{:S(2)}, u32[]{:S(2)}) %collective-permute-start.10) | collective-permute-done | bytes 2144 | tf_op jit(solution)/shard_map/ppermute | solution.py:18
  92.2 4.7 %collective-permute-start.15 = (f32[2,132,2]{2,1,0:T(8,128)S(1)}, f32[2,132,2]{2,1,0:T(8,128)S(1)}, u32[]{:S(2)}, u32[]{:S(2)}) collective-permute-start(f32[2,132,2]{2,1,0:T(8,128)S(1)} %get-tuple-element.29), channel_id=1, source_target_pairs={{1,0},{2,1},{3,2},{4,3},{5,4},{6,5},{7,6},{0,7},{9,8},{10,9},{11,1... | collective-permute-start | bytes 6344 | tf_op jit(solution)/shard_map/ppermute | solution.py:20
  97.1 4.2 %collective-permute-done.14 = f32[2,132,2]{2,1,0:T(8,128)S(1)} collective-permute-done((f32[2,132,2]{2,1,0:T(8,128)S(1)}, f32[2,132,2]{2,1,0:T(8,128)S(1)}, u32[]{:S(2)}, u32[]{:S(2)}) %collective-permute-start.14) | collective-permute-done | bytes 2144 | tf_op jit(solution)/shard_map/ppermute | solution.py:18
  105.9 5.1 %collective-permute-start.19 = (f32[2,132,2]{2,1,0:T(8,128)S(1)}, f32[2,132,2]{2,1,0:T(8,128)S(1)}, u32[]{:S(2)}, u32[]{:S(2)}) collective-permute-start(f32[2,132,2]{2,1,0:T(8,128)S(1)} %get-tuple-element.25), channel_id=1, source_target_pairs={{1,0},{2,1},{3,2},{4,3},{5,4},{6,5},{7,6},{0,7},{9,8},{10,9},{11,1... | collective-permute-start | bytes 6344 | tf_op jit(solution)/shard_map/ppermute | solution.py:20
  111.0 3.8 %collective-permute-done.18 = f32[2,132,2]{2,1,0:T(8,128)S(1)} collective-permute-done((f32[2,132,2]{2,1,0:T(8,128)S(1)}, f32[2,132,2]{2,1,0:T(8,128)S(1)}, u32[]{:S(2)}, u32[]{:S(2)}) %collective-permute-start.18) | collective-permute-done | bytes 2144 | tf_op jit(solution)/shard_map/ppermute | solution.py:18
  119.7 5.3 %collective-permute-start.23 = (f32[2,132,2]{2,1,0:T(8,128)S(1)}, f32[2,132,2]{2,1,0:T(8,128)S(1)}, u32[]{:S(2)}, u32[]{:S(2)}) collective-permute-start(f32[2,132,2]{2,1,0:T(8,128)S(1)} %get-tuple-element.21), channel_id=1, source_target_pairs={{1,0},{2,1},{3,2},{4,3},{5,4},{6,5},{7,6},{0,7},{9,8},{10,9},{11,1... | collective-permute-start | bytes 6344 | tf_op jit(solution)/shard_map/ppermute | solution.py:20
  125.1 3.9 %collective-permute-done.22 = f32[2,132,2]{2,1,0:T(8,128)S(1)} collective-permute-done((f32[2,132,2]{2,1,0:T(8,128)S(1)}, f32[2,132,2]{2,1,0:T(8,128)S(1)}, u32[]{:S(2)}, u32[]{:S(2)}) %collective-permute-start.22) | collective-permute-done | bytes 2144 | tf_op jit(solution)/shard_map/ppermute | solution.py:18
  134.7 4.5 %collective-permute-start.27 = (f32[2,132,2]{2,1,0:T(8,128)S(1)}, f32[2,132,2]{2,1,0:T(8,128)S(1)}, u32[]{:S(2)}, u32[]{:S(2)}) collective-permute-start(f32[2,132,2]{2,1,0:T(8,128)S(1)} %get-tuple-element.17), channel_id=1, source_target_pairs={{1,0},{2,1},{3,2},{4,3},{5,4},{6,5},{7,6},{0,7},{9,8},{10,9},{11,1... | collective-permute-start | bytes 6344 | tf_op jit(solution)/shard_map/ppermute | solution.py:20
  139.3 4.2 %collective-permute-done.26 = f32[2,132,2]{2,1,0:T(8,128)S(1)} collective-permute-done((f32[2,132,2]{2,1,0:T(8,128)S(1)}, f32[2,132,2]{2,1,0:T(8,128)S(1)}, u32[]{:S(2)}, u32[]{:S(2)}) %collective-permute-start.26) | collective-permute-done | bytes 2144 | tf_op jit(solution)/shard_map/ppermute | solution.py:18
  149.8 4.5 %collective-permute-start.31 = (f32[2,132,2]{2,1,0:T(8,128)S(1)}, f32[2,132,2]{2,1,0:T(8,128)S(1)}, u32[]{:S(2)}, u32[]{:S(2)}) collective-permute-start(f32[2,132,2]{2,1,0:T(8,128)S(1)} %get-tuple-element.13), channel_id=1, source_target_pairs={{1,0},{2,1},{3,2},{4,3},{5,4},{6,5},{7,6},{0,7},{9,8},{10,9},{11,1... | collective-permute-start | bytes 6344 | tf_op jit(solution)/shard_map/ppermute | solution.py:20
  154.5 4.0 %collective-permute-done.30 = f32[2,132,2]{2,1,0:T(8,128)S(1)} collective-permute-done((f32[2,132,2]{2,1,0:T(8,128)S(1)}, f32[2,132,2]{2,1,0:T(8,128)S(1)}, u32[]{:S(2)}, u32[]{:S(2)}) %collective-permute-start.30) | collective-permute-done | bytes 2144 | tf_op jit(solution)/shard_map/ppermute | solution.py:18
  (104 shorter events, 42.9 us)
Async XLA Ops:
  17.2 26.2 %all-to-all-start = ((bf16[8,2,20480]{2,1,0:T(2,128)(2,1)}), bf16[8,2,20480]{2,1,0:T(2,128)(2,1)S(1)}, u32[]{:S(2)}, u32[]{:S(2)}) async-start(bf16[8,2,20480]{2,1,0:T(2,128)(2,1)} %reshape.60), calls=%async_computation | async-start | bytes 1310720 | tf_op jit(solution)/shard_map/all_to_all | solution.py:50
  24.5 3.1 %collective-permute-start = (f32[2,2,512]{2,1,0:T(2,128)S(1)}, f32[2,2,512]{2,1,0:T(2,128)S(1)}, u32[]{:S(2)}, u32[]{:S(2)}) collective-permute-start(f32[2,2,512]{2,1,0:T(2,128)S(1)} %get-tuple-element.73), channel_id=1, source_target_pairs={{0,8},{8,16},{16,24},{24,0},{1,9},{9,17},{17,25},{25,1},{2,10},{10... | collective-permute-start | bytes 24584 | tf_op jit(solution)/shard_map/ppermute | solution.py:18
  27.8 15.4 %collective-permute-start.2 = (f32[2,132,2]{2,1,0:T(8,128)S(1)}, f32[2,132,2]{2,1,0:T(8,128)S(1)}, u32[]{:S(2)}, u32[]{:S(2)}) collective-permute-start(f32[2,132,2]{2,1,0:T(8,128)S(1)} %get-tuple-element.40), channel_id=1, source_target_pairs={{0,1},{1,2},{2,3},{3,4},{4,5},{5,6},{6,7},{7,0},{8,9},{9,10},{10,1... | collective-permute-start | bytes 6344 | tf_op jit(solution)/shard_map/ppermute | solution.py:18
  29.8 13.3 %collective-permute-start.3 = (f32[2,132,2]{2,1,0:T(8,128)S(1)}, f32[2,132,2]{2,1,0:T(8,128)S(1)}, u32[]{:S(2)}, u32[]{:S(2)}) collective-permute-start(f32[2,132,2]{2,1,0:T(8,128)S(1)} %get-tuple-element.41), channel_id=1, source_target_pairs={{1,0},{2,1},{3,2},{4,3},{5,4},{6,5},{7,6},{0,7},{9,8},{10,9},{11,1... | collective-permute-start | bytes 6344 | tf_op jit(solution)/shard_map/ppermute | solution.py:20
  58.2 3.1 %collective-permute-start.4 = (f32[2,2,512]{2,1,0:T(2,128)S(1)}, f32[2,2,512]{2,1,0:T(2,128)S(1)}, u32[]{:S(2)}, u32[]{:S(2)}) collective-permute-start(f32[2,2,512]{2,1,0:T(2,128)S(1)} %get-tuple-element.68), channel_id=1, source_target_pairs={{0,8},{8,16},{16,24},{24,0},{1,9},{9,17},{17,25},{25,1},{2,10},{10... | collective-permute-start | bytes 24584 | tf_op jit(solution)/shard_map/ppermute | solution.py:18
  61.5 9.3 %collective-permute-start.6 = (f32[2,132,2]{2,1,0:T(8,128)S(1)}, f32[2,132,2]{2,1,0:T(8,128)S(1)}, u32[]{:S(2)}, u32[]{:S(2)}) collective-permute-start(f32[2,132,2]{2,1,0:T(8,128)S(1)} %get-tuple-element.36), channel_id=1, source_target_pairs={{0,1},{1,2},{2,3},{3,4},{4,5},{5,6},{6,7},{7,0},{8,9},{9,10},{10,1... | collective-permute-start | bytes 6344 | tf_op jit(solution)/shard_map/ppermute | solution.py:18
  64.3 9.4 %collective-permute-start.7 = (f32[2,132,2]{2,1,0:T(8,128)S(1)}, f32[2,132,2]{2,1,0:T(8,128)S(1)}, u32[]{:S(2)}, u32[]{:S(2)}) collective-permute-start(f32[2,132,2]{2,1,0:T(8,128)S(1)} %get-tuple-element.37), channel_id=1, source_target_pairs={{1,0},{2,1},{3,2},{4,3},{5,4},{6,5},{7,6},{0,7},{9,8},{10,9},{11,1... | collective-permute-start | bytes 6344 | tf_op jit(solution)/shard_map/ppermute | solution.py:20
  74.9 3.1 %collective-permute-start.8 = (f32[2,2,512]{2,1,0:T(2,128)S(1)}, f32[2,2,512]{2,1,0:T(2,128)S(1)}, u32[]{:S(2)}, u32[]{:S(2)}) collective-permute-start(f32[2,2,512]{2,1,0:T(2,128)S(1)} %get-tuple-element.64), channel_id=1, source_target_pairs={{0,8},{8,16},{16,24},{24,0},{1,9},{9,17},{17,25},{25,1},{2,10},{10... | collective-permute-start | bytes 24584 | tf_op jit(solution)/shard_map/ppermute | solution.py:18
  78.2 9.3 %collective-permute-start.10 = (f32[2,132,2]{2,1,0:T(8,128)S(1)}, f32[2,132,2]{2,1,0:T(8,128)S(1)}, u32[]{:S(2)}, u32[]{:S(2)}) collective-permute-start(f32[2,132,2]{2,1,0:T(8,128)S(1)} %get-tuple-element.32), channel_id=1, source_target_pairs={{0,1},{1,2},{2,3},{3,4},{4,5},{5,6},{6,7},{7,0},{8,9},{9,10},{10,1... | collective-permute-start | bytes 6344 | tf_op jit(solution)/shard_map/ppermute | solution.py:18
  78.2 9.5 %collective-permute-start.11 = (f32[2,132,2]{2,1,0:T(8,128)S(1)}, f32[2,132,2]{2,1,0:T(8,128)S(1)}, u32[]{:S(2)}, u32[]{:S(2)}) collective-permute-start(f32[2,132,2]{2,1,0:T(8,128)S(1)} %get-tuple-element.33), channel_id=1, source_target_pairs={{1,0},{2,1},{3,2},{4,3},{5,4},{6,5},{7,6},{0,7},{9,8},{10,9},{11,1... | collective-permute-start | bytes 6344 | tf_op jit(solution)/shard_map/ppermute | solution.py:20
  88.8 3.1 %collective-permute-start.12 = (f32[2,2,512]{2,1,0:T(2,128)S(1)}, f32[2,2,512]{2,1,0:T(2,128)S(1)}, u32[]{:S(2)}, u32[]{:S(2)}) collective-permute-start(f32[2,2,512]{2,1,0:T(2,128)S(1)} %get-tuple-element.60), channel_id=1, source_target_pairs={{0,8},{8,16},{16,24},{24,0},{1,9},{9,17},{17,25},{25,1},{2,10},{10... | collective-permute-start | bytes 24584 | tf_op jit(solution)/shard_map/ppermute | solution.py:18
  92.1 9.1 %collective-permute-start.14 = (f32[2,132,2]{2,1,0:T(8,128)S(1)}, f32[2,132,2]{2,1,0:T(8,128)S(1)}, u32[]{:S(2)}, u32[]{:S(2)}) collective-permute-start(f32[2,132,2]{2,1,0:T(8,128)S(1)} %get-tuple-element.28), channel_id=1, source_target_pairs={{0,1},{1,2},{2,3},{3,4},{4,5},{5,6},{6,7},{7,0},{8,9},{9,10},{10,1... | collective-permute-start | bytes 6344 | tf_op jit(solution)/shard_map/ppermute | solution.py:18
  92.2 9.0 %collective-permute-start.15 = (f32[2,132,2]{2,1,0:T(8,128)S(1)}, f32[2,132,2]{2,1,0:T(8,128)S(1)}, u32[]{:S(2)}, u32[]{:S(2)}) collective-permute-start(f32[2,132,2]{2,1,0:T(8,128)S(1)} %get-tuple-element.29), channel_id=1, source_target_pairs={{1,0},{2,1},{3,2},{4,3},{5,4},{6,5},{7,6},{0,7},{9,8},{10,9},{11,1... | collective-permute-start | bytes 6344 | tf_op jit(solution)/shard_map/ppermute | solution.py:20
  102.5 3.1 %collective-permute-start.16 = (f32[2,2,512]{2,1,0:T(2,128)S(1)}, f32[2,2,512]{2,1,0:T(2,128)S(1)}, u32[]{:S(2)}, u32[]{:S(2)}) collective-permute-start(f32[2,2,512]{2,1,0:T(2,128)S(1)} %get-tuple-element.56), channel_id=1, source_target_pairs={{0,8},{8,16},{16,24},{24,0},{1,9},{9,17},{17,25},{25,1},{2,10},{10... | collective-permute-start | bytes 24584 | tf_op jit(solution)/shard_map/ppermute | solution.py:18
  105.8 9.0 %collective-permute-start.18 = (f32[2,132,2]{2,1,0:T(8,128)S(1)}, f32[2,132,2]{2,1,0:T(8,128)S(1)}, u32[]{:S(2)}, u32[]{:S(2)}) collective-permute-start(f32[2,132,2]{2,1,0:T(8,128)S(1)} %get-tuple-element.24), channel_id=1, source_target_pairs={{0,1},{1,2},{2,3},{3,4},{4,5},{5,6},{6,7},{7,0},{8,9},{9,10},{10,1... | collective-permute-start | bytes 6344 | tf_op jit(solution)/shard_map/ppermute | solution.py:18
  105.9 9.1 %collective-permute-start.19 = (f32[2,132,2]{2,1,0:T(8,128)S(1)}, f32[2,132,2]{2,1,0:T(8,128)S(1)}, u32[]{:S(2)}, u32[]{:S(2)}) collective-permute-start(f32[2,132,2]{2,1,0:T(8,128)S(1)} %get-tuple-element.25), channel_id=1, source_target_pairs={{1,0},{2,1},{3,2},{4,3},{5,4},{6,5},{7,6},{0,7},{9,8},{10,9},{11,1... | collective-permute-start | bytes 6344 | tf_op jit(solution)/shard_map/ppermute | solution.py:20
  116.3 3.1 %collective-permute-start.20 = (f32[2,2,512]{2,1,0:T(2,128)S(1)}, f32[2,2,512]{2,1,0:T(2,128)S(1)}, u32[]{:S(2)}, u32[]{:S(2)}) collective-permute-start(f32[2,2,512]{2,1,0:T(2,128)S(1)} %get-tuple-element.52), channel_id=1, source_target_pairs={{0,8},{8,16},{16,24},{24,0},{1,9},{9,17},{17,25},{25,1},{2,10},{10... | collective-permute-start | bytes 24584 | tf_op jit(solution)/shard_map/ppermute | solution.py:18
  119.6 9.4 %collective-permute-start.22 = (f32[2,132,2]{2,1,0:T(8,128)S(1)}, f32[2,132,2]{2,1,0:T(8,128)S(1)}, u32[]{:S(2)}, u32[]{:S(2)}) collective-permute-start(f32[2,132,2]{2,1,0:T(8,128)S(1)} %get-tuple-element.20), channel_id=1, source_target_pairs={{0,1},{1,2},{2,3},{3,4},{4,5},{5,6},{6,7},{7,0},{8,9},{9,10},{10,1... | collective-permute-start | bytes 6344 | tf_op jit(solution)/shard_map/ppermute | solution.py:18
  119.7 10.2 %collective-permute-start.23 = (f32[2,132,2]{2,1,0:T(8,128)S(1)}, f32[2,132,2]{2,1,0:T(8,128)S(1)}, u32[]{:S(2)}, u32[]{:S(2)}) collective-permute-start(f32[2,132,2]{2,1,0:T(8,128)S(1)} %get-tuple-element.21), channel_id=1, source_target_pairs={{1,0},{2,1},{3,2},{4,3},{5,4},{6,5},{7,6},{0,7},{9,8},{10,9},{11,1... | collective-permute-start | bytes 6344 | tf_op jit(solution)/shard_map/ppermute | solution.py:20
  131.2 3.1 %collective-permute-start.24 = (f32[2,2,512]{2,1,0:T(2,128)S(1)}, f32[2,2,512]{2,1,0:T(2,128)S(1)}, u32[]{:S(2)}, u32[]{:S(2)}) collective-permute-start(f32[2,2,512]{2,1,0:T(2,128)S(1)} %get-tuple-element.48), channel_id=1, source_target_pairs={{0,8},{8,16},{16,24},{24,0},{1,9},{9,17},{17,25},{25,1},{2,10},{10... | collective-permute-start | bytes 24584 | tf_op jit(solution)/shard_map/ppermute | solution.py:18
  134.5 9.0 %collective-permute-start.26 = (f32[2,132,2]{2,1,0:T(8,128)S(1)}, f32[2,132,2]{2,1,0:T(8,128)S(1)}, u32[]{:S(2)}, u32[]{:S(2)}) collective-permute-start(f32[2,132,2]{2,1,0:T(8,128)S(1)} %get-tuple-element.16), channel_id=1, source_target_pairs={{0,1},{1,2},{2,3},{3,4},{4,5},{5,6},{6,7},{7,0},{8,9},{9,10},{10,1... | collective-permute-start | bytes 6344 | tf_op jit(solution)/shard_map/ppermute | solution.py:18
  134.7 10.2 %collective-permute-start.27 = (f32[2,132,2]{2,1,0:T(8,128)S(1)}, f32[2,132,2]{2,1,0:T(8,128)S(1)}, u32[]{:S(2)}, u32[]{:S(2)}) collective-permute-start(f32[2,132,2]{2,1,0:T(8,128)S(1)} %get-tuple-element.17), channel_id=1, source_target_pairs={{1,0},{2,1},{3,2},{4,3},{5,4},{6,5},{7,6},{0,7},{9,8},{10,9},{11,1... | collective-permute-start | bytes 6344 | tf_op jit(solution)/shard_map/ppermute | solution.py:20
  149.6 9.0 %collective-permute-start.30 = (f32[2,132,2]{2,1,0:T(8,128)S(1)}, f32[2,132,2]{2,1,0:T(8,128)S(1)}, u32[]{:S(2)}, u32[]{:S(2)}) collective-permute-start(f32[2,132,2]{2,1,0:T(8,128)S(1)} %get-tuple-element.12), channel_id=1, source_target_pairs={{0,1},{1,2},{2,3},{3,4},{4,5},{5,6},{6,7},{7,0},{8,9},{9,10},{10,1... | collective-permute-start | bytes 6344 | tf_op jit(solution)/shard_map/ppermute | solution.py:18
  149.8 10.2 %collective-permute-start.31 = (f32[2,132,2]{2,1,0:T(8,128)S(1)}, f32[2,132,2]{2,1,0:T(8,128)S(1)}, u32[]{:S(2)}, u32[]{:S(2)}) collective-permute-start(f32[2,132,2]{2,1,0:T(8,128)S(1)} %get-tuple-element.13), channel_id=1, source_target_pairs={{1,0},{2,1},{3,2},{4,3},{5,4},{6,5},{7,6},{0,7},{9,8},{10,9},{11,1... | collective-permute-start | bytes 6344 | tf_op jit(solution)/shard_map/ppermute | solution.py:20
  (10 other events, 51.2 us)
where the time goes:
time: 163 us; the launch traced here: 162 us
  starting transfers between devices  60.8 us (37%)
  waiting for transfers between devices  57.7 us (35%)
  local copies, waits for them, and re-layouts  31.8 us (20%)
  other arithmetic  11.7 us (7%)
    ppermute x16, waiting for transfers between devices, with_halo(): lax.ppermute(tail, axis, [(i, (i + 1) % count) for i in range(count)])  50.1 us
    ppermute x16, starting transfers between devices, with_halo(): lax.ppermute(head, axis, [((i + 1) % count, i) for i in range(count)])  46.3 us
    unnamed x6, local copies, waits for them, and re-layouts  24.5 us
    ppermute x16, waiting for transfers between devices, with_halo(): lax.ppermute(head, axis, [((i + 1) % count, i) for i in range(count)])  7.54 us
    ppermute x16, starting transfers between devices, with_halo(): lax.ppermute(tail, axis, [(i, (i + 1) % count) for i in range(count)])  7.29 us
    all_to_all x1, starting transfers between devices, local(): lax.all_to_all(index_panels, 'col', split_axis=2, concat_axis=1, tiled=True)  7.28 us
    all_to_all x1, local copies, waits for them, and re-layouts, local(): lax.all_to_all(index_panels, 'col', split_axis=2, concat_axis=1, tiled=True)  6.41 us
    add x8, other arithmetic, slope(): diffraction * laplace(padded)  4.96 us
  transfers between devices with their start and end apart: 33, of which 22 were waited for; matrix products, arithmetic and copies ran while one was open for 1% of the time, Pallas kernels for 0%

commit v1 on v0

--- a/solution.py
+++ b/solution.py
@@ -6,6 +6,18 @@
 STEPS = 2
 diffraction = 0.15
 phase_gain = 0.25
+
+
+def cut_along(shard, dim, size):
+    shape = shard.shape
+    blocks = shard.reshape(*shape[:dim], size, shape[dim] // size, *shape[dim + 1 :])
+    return jnp.moveaxis(blocks, dim, 0)
+
+
+def in_order(blocks, dim):
+    shape = list(blocks.shape[1:])
+    shape[dim] *= blocks.shape[0]
+    return jnp.moveaxis(blocks, 0, dim).reshape(shape)
 
 
 def with_halo(cells, sides, width):
@@ -47,7 +59,14 @@
 
 
 def local(optical_field, index_panels):
-    planes_all = lax.all_to_all(index_panels, "col", split_axis=2, concat_axis=1, tiled=True)
+    size, mine = (lax.axis_size("col"), lax.axis_index("col"))
+    blocks = cut_along(index_panels, 2, size)
+    finished = [blocks[mine]]
+    for lap in range(1, size):
+        sent = blocks[mine ^ lap]
+        finished.append(lax.ppermute(sent, "col", [(i_2, i_2 ^ lap) for i_2 in range(size)]))
+    blocks = jnp.stack(finished)[mine ^ jnp.arange(size)]
+    planes_all = in_order(blocks, 1)
     field = optical_field
     planes = None
     for step_index in range(STEPS):

time: 163 us -> 145 us (0.89)
  local copies, waits for them, and re-layouts: 31.8 us -> 10.6 us
  starting transfers between devices: 60.8 us -> 65.5 us
    unnamed x6 -> x18, local copies, waits for them, and re-layouts: 24.5 us -> 5.9 us
    ppermute x0 -> x7, starting transfers between devices: none -> 12 us  [local(): lax.ppermute(sent, 'col', [(i_2, i_2 ^ lap) for i_2 in range(size)])]
    ppermute x16, waiting for transfers between devices: 50.1 us -> 41.8 us  [with_halo(): lax.ppermute(tail, axis, [(i, (i + 1) % count) for i in range(count)])]
    all_to_all x1 -> x0, starting transfers between devices: 7.28 us -> none  [local(): lax.all_to_all(index_panels, 'col', split_axis=2, concat_axis=1, tiled=True)]
    all_to_all x1 -> x0, local copies, waits for them, and re-layouts: 6.41 us -> none  [local(): lax.all_to_all(index_panels, 'col', split_axis=2, concat_axis=1, tiled=True)]
    ppermute x0 -> x7, waiting for transfers between devices: none -> 4.96 us  [local(): lax.ppermute(sent, 'col', [(i_2, i_2 ^ lap) for i_2 in range(size)])]
    another operation x0 -> x2, local copies, waits for them, and re-layouts: none -> 2.22 us
    ppermute x16, waiting for transfers between devices: 7.54 us -> 9.55 us  [with_halo(): lax.ppermute(head, axis, [((i + 1) % count, i) for i in range(count)])]
  transfers between devices with their start and end apart: 33 -> 39, of which waited for: 22 -> 23; matrix products, arithmetic and copies ran while one was open for 1% -> 5% of each run, Pallas kernels for 0% -> 0%
where the time goes in v1:
time: 145 us
  starting transfers between devices  65.5 us (45%)
  waiting for transfers between devices  56.3 us (39%)
  other arithmetic  11.7 us (8%)
  local copies, waits for them, and re-layouts  10.6 us (7%)
    ppermute x16, starting transfers between devices, with_halo(): lax.ppermute(head, axis, [((i + 1) % count, i) for i in range(count)])  47.6 us
    ppermute x16, waiting for transfers between devices, with_halo(): lax.ppermute(tail, axis, [(i, (i + 1) % count) for i in range(count)])  41.8 us
    ppermute x7, starting transfers between devices, local(): lax.ppermute(sent, 'col', [(i_2, i_2 ^ lap) for i_2 in range(size)])  12 us
    ppermute x16, waiting for transfers between devices, with_halo(): lax.ppermute(head, axis, [((i + 1) % count, i) for i in range(count)])  9.55 us
    ppermute x16, starting transfers between devices, with_halo(): lax.ppermute(tail, axis, [(i, (i + 1) % count) for i in range(count)])  5.95 us
    unnamed x18, local copies, waits for them, and re-layouts  5.9 us
    add x8, other arithmetic, slope(): diffraction * laplace(padded)  4.96 us
    ppermute x7, waiting for transfers between devices, local(): lax.ppermute(sent, 'col', [(i_2, i_2 ^ lap) for i_2 in range(size)])  4.96 us
  transfers between devices with their start and end apart: 39, of which 23 were waited for; matrix products, arithmetic and copies ran while one was open for 5% of the time, Pallas kernels for 0%

profile of v1, /device:TPU:0, one launch (start us, length us, event | category | flops | bytes accessed | tf_op | source)
XLA Modules:
  0.0 144.7 jit_solution(11211464724781880597)
XLA Ops:
  0.8 2.4 %collective-permute-start.1 = (f32[2,2,512]{2,1,0:T(2,128)S(1)}, f32[2,2,512]{2,1,0:T(2,128)S(1)}, u32[]{:S(2)}, u32[]{:S(2)}) collective-permute-start(f32[2,2,512]{2,1,0:T(2,128)S(1)} %get-tuple-element.80), channel_id=1, source_target_pairs={{8,0},{16,8},{24,16},{0,24},{9,1},{17,9},{25,17},{1,25},{10,2},{18... | collective-permute-start | bytes 24584 | tf_op jit(solution)/shard_map/ppermute | solution.py:32
  12.4 3.2 %collective-permute-start.3 = (f32[2,132,2]{2,1,0:T(8,128)S(1)}, f32[2,132,2]{2,1,0:T(8,128)S(1)}, u32[]{:S(2)}, u32[]{:S(2)}) collective-permute-start(f32[2,132,2]{2,1,0:T(8,128)S(1)} %get-tuple-element.49), channel_id=1, source_target_pairs={{1,0},{2,1},{3,2},{4,3},{5,4},{6,5},{7,6},{0,7},{9,8},{10,9},{11,1... | collective-permute-start | bytes 6344 | tf_op jit(solution)/shard_map/ppermute | solution.py:32
  15.6 4.4 %collective-permute-done.2 = f32[2,132,2]{2,1,0:T(8,128)S(1)} collective-permute-done((f32[2,132,2]{2,1,0:T(8,128)S(1)}, f32[2,132,2]{2,1,0:T(8,128)S(1)}, u32[]{:S(2)}, u32[]{:S(2)}) %collective-permute-start.2) | collective-permute-done | bytes 2144 | tf_op jit(solution)/shard_map/ppermute | solution.py:30
  20.1 1.9 %collective-permute-start.7 = (bf16[5,16,512]{2,1,0:T(8,128)(2,1)S(1)}, bf16[5,16,512]{2,1,0:T(8,128)(2,1)S(1)}, u32[]{:S(2)}, u32[]{:S(2)}) collective-permute-start(bf16[5,16,512]{2,1,0:T(8,128)(2,1)S(1)} %bitcast.66), channel_id=1, source_target_pairs={{0,4},{1,5},{2,6},{3,7},{4,0},{5,1},{6,2},{7,3},{8,12},{9,13},{10,... | collective-permute-start | bytes 245768 | tf_op jit(solution)/shard_map/ppermute | solution.py:67
  22.0 2.3 %collective-permute-start.8 = (bf16[5,16,512]{2,1,0:T(8,128)(2,1)S(1)}, bf16[5,16,512]{2,1,0:T(8,128)(2,1)S(1)}, u32[]{:S(2)}, u32[]{:S(2)}) collective-permute-start(bf16[5,16,512]{2,1,0:T(8,128)(2,1)S(1)} %bitcast.63), channel_id=1, source_target_pairs={{0,5},{1,4},{2,7},{3,6},{4,1},{5,0},{6,3},{7,2},{8,13},{9,12},{10,... | collective-permute-start | bytes 245768 | tf_op jit(solution)/shard_map/ppermute | solution.py:67
  24.5 3.7 %collective-permute-start.9 = (bf16[5,16,512]{2,1,0:T(8,128)(2,1)S(1)}, bf16[5,16,512]{2,1,0:T(8,128)(2,1)S(1)}, u32[]{:S(2)}, u32[]{:S(2)}) collective-permute-start(bf16[5,16,512]{2,1,0:T(8,128)(2,1)S(1)} %bitcast.61), channel_id=1, source_target_pairs={{0,6},{1,7},{2,4},{3,5},{4,2},{5,3},{6,0},{7,1},{8,14},{9,15},{10,... | collective-permute-start | bytes 245768 | tf_op jit(solution)/shard_map/ppermute | solution.py:67
  31.2 4.9 %collective-permute-done.8 = bf16[5,16,512]{2,1,0:T(8,128)(2,1)S(1)} collective-permute-done((bf16[5,16,512]{2,1,0:T(8,128)(2,1)S(1)}, bf16[5,16,512]{2,1,0:T(8,128)(2,1)S(1)}, u32[]{:S(2)}, u32[]{:S(2)}) %collective-permute-start.8) | collective-permute-done | bytes 81952 | tf_op jit(solution)/shard_map/ppermute | solution.py:67
  40.7 1.7 %collective-permute-start.12 = (f32[2,2,512]{2,1,0:T(2,128)S(1)}, f32[2,2,512]{2,1,0:T(2,128)S(1)}, u32[]{:S(2)}, u32[]{:S(2)}) collective-permute-start(f32[2,2,512]{2,1,0:T(2,128)S(1)} %get-tuple-element.77), channel_id=1, source_target_pairs={{8,0},{16,8},{24,16},{0,24},{9,1},{17,9},{25,17},{1,25},{10,2},{18... | collective-permute-start | bytes 24584 | tf_op jit(solution)/shard_map/ppermute | solution.py:32
  44.6 4.1 %collective-permute-start.14 = (f32[2,132,2]{2,1,0:T(8,128)S(1)}, f32[2,132,2]{2,1,0:T(8,128)S(1)}, u32[]{:S(2)}, u32[]{:S(2)}) collective-permute-start(f32[2,132,2]{2,1,0:T(8,128)S(1)} %get-tuple-element.45), channel_id=1, source_target_pairs={{1,0},{2,1},{3,2},{4,3},{5,4},{6,5},{7,6},{0,7},{9,8},{10,9},{11,1... | collective-permute-start | bytes 6344 | tf_op jit(solution)/shard_map/ppermute | solution.py:32
  48.7 4.2 %collective-permute-done.13 = f32[2,132,2]{2,1,0:T(8,128)S(1)} collective-permute-done((f32[2,132,2]{2,1,0:T(8,128)S(1)}, f32[2,132,2]{2,1,0:T(8,128)S(1)}, u32[]{:S(2)}, u32[]{:S(2)}) %collective-permute-start.13) | collective-permute-done | bytes 2144 | tf_op jit(solution)/shard_map/ppermute | solution.py:30
  59.2 4.6 %collective-permute-start.18 = (f32[2,132,2]{2,1,0:T(8,128)S(1)}, f32[2,132,2]{2,1,0:T(8,128)S(1)}, u32[]{:S(2)}, u32[]{:S(2)}) collective-permute-start(f32[2,132,2]{2,1,0:T(8,128)S(1)} %get-tuple-element.41), channel_id=1, source_target_pairs={{1,0},{2,1},{3,2},{4,3},{5,4},{6,5},{7,6},{0,7},{9,8},{10,9},{11,1... | collective-permute-start | bytes 6344 | tf_op jit(solution)/shard_map/ppermute | solution.py:32
  63.8 4.0 %collective-permute-done.17 = f32[2,132,2]{2,1,0:T(8,128)S(1)} collective-permute-done((f32[2,132,2]{2,1,0:T(8,128)S(1)}, f32[2,132,2]{2,1,0:T(8,128)S(1)}, u32[]{:S(2)}, u32[]{:S(2)}) %collective-permute-start.17) | collective-permute-done | bytes 2144 | tf_op jit(solution)/shard_map/ppermute | solution.py:30
  67.8 1.8 %collective-permute-done.18 = f32[2,132,2]{2,1,0:T(8,128)S(1)} collective-permute-done((f32[2,132,2]{2,1,0:T(8,128)S(1)}, f32[2,132,2]{2,1,0:T(8,128)S(1)}, u32[]{:S(2)}, u32[]{:S(2)}) %collective-permute-start.18) | collective-permute-done | bytes 2144 | tf_op jit(solution)/shard_map/ppermute | solution.py:32
  74.2 4.5 %collective-permute-start.22 = (f32[2,132,2]{2,1,0:T(8,128)S(1)}, f32[2,132,2]{2,1,0:T(8,128)S(1)}, u32[]{:S(2)}, u32[]{:S(2)}) collective-permute-start(f32[2,132,2]{2,1,0:T(8,128)S(1)} %get-tuple-element.37), channel_id=1, source_target_pairs={{1,0},{2,1},{3,2},{4,3},{5,4},{6,5},{7,6},{0,7},{9,8},{10,9},{11,1... | collective-permute-start | bytes 6344 | tf_op jit(solution)/shard_map/ppermute | solution.py:32
  78.7 4.1 %collective-permute-done.21 = f32[2,132,2]{2,1,0:T(8,128)S(1)} collective-permute-done((f32[2,132,2]{2,1,0:T(8,128)S(1)}, f32[2,132,2]{2,1,0:T(8,128)S(1)}, u32[]{:S(2)}, u32[]{:S(2)}) %collective-permute-start.21) | collective-permute-done | bytes 2144 | tf_op jit(solution)/shard_map/ppermute | solution.py:30
  88.8 4.6 %collective-permute-start.26 = (f32[2,132,2]{2,1,0:T(8,128)S(1)}, f32[2,132,2]{2,1,0:T(8,128)S(1)}, u32[]{:S(2)}, u32[]{:S(2)}) collective-permute-start(f32[2,132,2]{2,1,0:T(8,128)S(1)} %get-tuple-element.33), channel_id=1, source_target_pairs={{1,0},{2,1},{3,2},{4,3},{5,4},{6,5},{7,6},{0,7},{9,8},{10,9},{11,1... | collective-permute-start | bytes 6344 | tf_op jit(solution)/shard_map/ppermute | solution.py:32
  93.4 4.1 %collective-permute-done.25 = f32[2,132,2]{2,1,0:T(8,128)S(1)} collective-permute-done((f32[2,132,2]{2,1,0:T(8,128)S(1)}, f32[2,132,2]{2,1,0:T(8,128)S(1)}, u32[]{:S(2)}, u32[]{:S(2)}) %collective-permute-start.25) | collective-permute-done | bytes 2144 | tf_op jit(solution)/shard_map/ppermute | solution.py:30
  102.8 4.6 %collective-permute-start.30 = (f32[2,132,2]{2,1,0:T(8,128)S(1)}, f32[2,132,2]{2,1,0:T(8,128)S(1)}, u32[]{:S(2)}, u32[]{:S(2)}) collective-permute-start(f32[2,132,2]{2,1,0:T(8,128)S(1)} %get-tuple-element.29), channel_id=1, source_target_pairs={{1,0},{2,1},{3,2},{4,3},{5,4},{6,5},{7,6},{0,7},{9,8},{10,9},{11,1... | collective-permute-start | bytes 6344 | tf_op jit(solution)/shard_map/ppermute | solution.py:32
  107.3 3.5 %collective-permute-done.29 = f32[2,132,2]{2,1,0:T(8,128)S(1)} collective-permute-done((f32[2,132,2]{2,1,0:T(8,128)S(1)}, f32[2,132,2]{2,1,0:T(8,128)S(1)}, u32[]{:S(2)}, u32[]{:S(2)}) %collective-permute-start.29) | collective-permute-done | bytes 2144 | tf_op jit(solution)/shard_map/ppermute | solution.py:30
  116.7 4.5 %collective-permute-start.34 = (f32[2,132,2]{2,1,0:T(8,128)S(1)}, f32[2,132,2]{2,1,0:T(8,128)S(1)}, u32[]{:S(2)}, u32[]{:S(2)}) collective-permute-start(f32[2,132,2]{2,1,0:T(8,128)S(1)} %get-tuple-element.25), channel_id=1, source_target_pairs={{1,0},{2,1},{3,2},{4,3},{5,4},{6,5},{7,6},{0,7},{9,8},{10,9},{11,1... | collective-permute-start | bytes 6344 | tf_op jit(solution)/shard_map/ppermute | solution.py:32
  121.2 3.8 %collective-permute-done.33 = f32[2,132,2]{2,1,0:T(8,128)S(1)} collective-permute-done((f32[2,132,2]{2,1,0:T(8,128)S(1)}, f32[2,132,2]{2,1,0:T(8,128)S(1)}, u32[]{:S(2)}, u32[]{:S(2)}) %collective-permute-start.33) | collective-permute-done | bytes 2144 | tf_op jit(solution)/shard_map/ppermute | solution.py:30
  125.1 2.2 %collective-permute-done.34 = f32[2,132,2]{2,1,0:T(8,128)S(1)} collective-permute-done((f32[2,132,2]{2,1,0:T(8,128)S(1)}, f32[2,132,2]{2,1,0:T(8,128)S(1)}, u32[]{:S(2)}, u32[]{:S(2)}) %collective-permute-start.34) | collective-permute-done | bytes 2144 | tf_op jit(solution)/shard_map/ppermute | solution.py:32
  132.1 4.5 %collective-permute-start.38 = (f32[2,132,2]{2,1,0:T(8,128)S(1)}, f32[2,132,2]{2,1,0:T(8,128)S(1)}, u32[]{:S(2)}, u32[]{:S(2)}) collective-permute-start(f32[2,132,2]{2,1,0:T(8,128)S(1)} %get-tuple-element.21), channel_id=1, source_target_pairs={{1,0},{2,1},{3,2},{4,3},{5,4},{6,5},{7,6},{0,7},{9,8},{10,9},{11,1... | collective-permute-start | bytes 6344 | tf_op jit(solution)/shard_map/ppermute | solution.py:32
  136.7 4.2 %collective-permute-done.37 = f32[2,132,2]{2,1,0:T(8,128)S(1)} collective-permute-done((f32[2,132,2]{2,1,0:T(8,128)S(1)}, f32[2,132,2]{2,1,0:T(8,128)S(1)}, u32[]{:S(2)}, u32[]{:S(2)}) %collective-permute-start.37) | collective-permute-done | bytes 2144 | tf_op jit(solution)/shard_map/ppermute | solution.py:30
  (127 shorter events, 56.2 us)
Async XLA Ops:
  0.8 9.9 %collective-permute-start.1 = (f32[2,2,512]{2,1,0:T(2,128)S(1)}, f32[2,2,512]{2,1,0:T(2,128)S(1)}, u32[]{:S(2)}, u32[]{:S(2)}) collective-permute-start(f32[2,2,512]{2,1,0:T(2,128)S(1)} %get-tuple-element.80), channel_id=1, source_target_pairs={{8,0},{16,8},{24,16},{0,24},{9,1},{17,9},{25,17},{1,25},{10,2},{18... | collective-permute-start | bytes 24584 | tf_op jit(solution)/shard_map/ppermute | solution.py:32
  6.2 18.3 %collective-permute-start.4 = (bf16[5,16,512]{2,1,0:T(8,128)(2,1)S(1)}, bf16[5,16,512]{2,1,0:T(8,128)(2,1)S(1)}, u32[]{:S(2)}, u32[]{:S(2)}) collective-permute-start(bf16[5,16,512]{2,1,0:T(8,128)(2,1)S(1)} %bitcast.65), channel_id=1, source_target_pairs={{0,1},{1,0},{2,3},{3,2},{4,5},{5,4},{6,7},{7,6},{8,9},{9,8},{10,11... | collective-permute-start | bytes 245768 | tf_op jit(solution)/shard_map/ppermute | solution.py:67
  7.8 21.0 %collective-permute-start.5 = (bf16[5,16,512]{2,1,0:T(8,128)(2,1)S(1)}, bf16[5,16,512]{2,1,0:T(8,128)(2,1)S(1)}, u32[]{:S(2)}, u32[]{:S(2)}) collective-permute-start(bf16[5,16,512]{2,1,0:T(8,128)(2,1)S(1)} %bitcast.64), channel_id=1, source_target_pairs={{0,2},{1,3},{2,0},{3,1},{4,6},{5,7},{6,4},{7,5},{8,10},{9,11},{10,... | collective-permute-start | bytes 245768 | tf_op jit(solution)/shard_map/ppermute | solution.py:67
  9.4 20.5 %collective-permute-start.6 = (bf16[5,16,512]{2,1,0:T(8,128)(2,1)S(1)}, bf16[5,16,512]{2,1,0:T(8,128)(2,1)S(1)}, u32[]{:S(2)}, u32[]{:S(2)}) collective-permute-start(bf16[5,16,512]{2,1,0:T(8,128)(2,1)S(1)} %bitcast.62), channel_id=1, source_target_pairs={{0,3},{1,2},{2,1},{3,0},{4,7},{5,6},{6,5},{7,4},{8,11},{9,10},{10,... | collective-permute-start | bytes 245768 | tf_op jit(solution)/shard_map/ppermute | solution.py:67
  10.8 9.2 %collective-permute-start.2 = (f32[2,132,2]{2,1,0:T(8,128)S(1)}, f32[2,132,2]{2,1,0:T(8,128)S(1)}, u32[]{:S(2)}, u32[]{:S(2)}) collective-permute-start(f32[2,132,2]{2,1,0:T(8,128)S(1)} %get-tuple-element.48), channel_id=1, source_target_pairs={{0,1},{1,2},{2,3},{3,4},{4,5},{5,6},{6,7},{7,0},{8,9},{9,10},{10,1... | collective-permute-start | bytes 6344 | tf_op jit(solution)/shard_map/ppermute | solution.py:30
  12.4 9.5 %collective-permute-start.3 = (f32[2,132,2]{2,1,0:T(8,128)S(1)}, f32[2,132,2]{2,1,0:T(8,128)S(1)}, u32[]{:S(2)}, u32[]{:S(2)}) collective-permute-start(f32[2,132,2]{2,1,0:T(8,128)S(1)} %get-tuple-element.49), channel_id=1, source_target_pairs={{1,0},{2,1},{3,2},{4,3},{5,4},{6,5},{7,6},{0,7},{9,8},{10,9},{11,1... | collective-permute-start | bytes 6344 | tf_op jit(solution)/shard_map/ppermute | solution.py:32
  20.1 10.5 %collective-permute-start.7 = (bf16[5,16,512]{2,1,0:T(8,128)(2,1)S(1)}, bf16[5,16,512]{2,1,0:T(8,128)(2,1)S(1)}, u32[]{:S(2)}, u32[]{:S(2)}) collective-permute-start(bf16[5,16,512]{2,1,0:T(8,128)(2,1)S(1)} %bitcast.66), channel_id=1, source_target_pairs={{0,4},{1,5},{2,6},{3,7},{4,0},{5,1},{6,2},{7,3},{8,12},{9,13},{10,... | collective-permute-start | bytes 245768 | tf_op jit(solution)/shard_map/ppermute | solution.py:67
  22.0 14.2 %collective-permute-start.8 = (bf16[5,16,512]{2,1,0:T(8,128)(2,1)S(1)}, bf16[5,16,512]{2,1,0:T(8,128)(2,1)S(1)}, u32[]{:S(2)}, u32[]{:S(2)}) collective-permute-start(bf16[5,16,512]{2,1,0:T(8,128)(2,1)S(1)} %bitcast.63), channel_id=1, source_target_pairs={{0,5},{1,4},{2,7},{3,6},{4,1},{5,0},{6,3},{7,2},{8,13},{9,12},{10,... | collective-permute-start | bytes 245768 | tf_op jit(solution)/shard_map/ppermute | solution.py:67
  24.5 12.2 %collective-permute-start.9 = (bf16[5,16,512]{2,1,0:T(8,128)(2,1)S(1)}, bf16[5,16,512]{2,1,0:T(8,128)(2,1)S(1)}, u32[]{:S(2)}, u32[]{:S(2)}) collective-permute-start(bf16[5,16,512]{2,1,0:T(8,128)(2,1)S(1)} %bitcast.61), channel_id=1, source_target_pairs={{0,6},{1,7},{2,4},{3,5},{4,2},{5,3},{6,0},{7,1},{8,14},{9,15},{10,... | collective-permute-start | bytes 245768 | tf_op jit(solution)/shard_map/ppermute | solution.py:67
  28.8 8.6 %collective-permute-start.10 = (bf16[5,16,512]{2,1,0:T(8,128)(2,1)S(1)}, bf16[5,16,512]{2,1,0:T(8,128)(2,1)S(1)}, u32[]{:S(2)}, u32[]{:S(2)}) collective-permute-start(bf16[5,16,512]{2,1,0:T(8,128)(2,1)S(1)} %bitcast.60), channel_id=1, source_target_pairs={{0,7},{1,6},{2,5},{3,4},{4,3},{5,2},{6,1},{7,0},{8,15},{9,14},{10,... | collective-permute-start | bytes 245768 | tf_op jit(solution)/shard_map/ppermute | solution.py:67
  44.0 9.0 %collective-permute-start.13 = (f32[2,132,2]{2,1,0:T(8,128)S(1)}, f32[2,132,2]{2,1,0:T(8,128)S(1)}, u32[]{:S(2)}, u32[]{:S(2)}) collective-permute-start(f32[2,132,2]{2,1,0:T(8,128)S(1)} %get-tuple-element.44), channel_id=1, source_target_pairs={{0,1},{1,2},{2,3},{3,4},{4,5},{5,6},{6,7},{7,0},{8,9},{9,10},{10,1... | collective-permute-start | bytes 6344 | tf_op jit(solution)/shard_map/ppermute | solution.py:30
  44.6 10.0 %collective-permute-start.14 = (f32[2,132,2]{2,1,0:T(8,128)S(1)}, f32[2,132,2]{2,1,0:T(8,128)S(1)}, u32[]{:S(2)}, u32[]{:S(2)}) collective-permute-start(f32[2,132,2]{2,1,0:T(8,128)S(1)} %get-tuple-element.45), channel_id=1, source_target_pairs={{1,0},{2,1},{3,2},{4,3},{5,4},{6,5},{7,6},{0,7},{9,8},{10,9},{11,1... | collective-permute-start | bytes 6344 | tf_op jit(solution)/shard_map/ppermute | solution.py:32
  59.0 8.8 %collective-permute-start.17 = (f32[2,132,2]{2,1,0:T(8,128)S(1)}, f32[2,132,2]{2,1,0:T(8,128)S(1)}, u32[]{:S(2)}, u32[]{:S(2)}) collective-permute-start(f32[2,132,2]{2,1,0:T(8,128)S(1)} %get-tuple-element.40), channel_id=1, source_target_pairs={{0,1},{1,2},{2,3},{3,4},{4,5},{5,6},{6,7},{7,0},{8,9},{9,10},{10,1... | collective-permute-start | bytes 6344 | tf_op jit(solution)/shard_map/ppermute | solution.py:30
  59.2 10.4 %collective-permute-start.18 = (f32[2,132,2]{2,1,0:T(8,128)S(1)}, f32[2,132,2]{2,1,0:T(8,128)S(1)}, u32[]{:S(2)}, u32[]{:S(2)}) collective-permute-start(f32[2,132,2]{2,1,0:T(8,128)S(1)} %get-tuple-element.41), channel_id=1, source_target_pairs={{1,0},{2,1},{3,2},{4,3},{5,4},{6,5},{7,6},{0,7},{9,8},{10,9},{11,1... | collective-permute-start | bytes 6344 | tf_op jit(solution)/shard_map/ppermute | solution.py:32
  73.9 8.9 %collective-permute-start.21 = (f32[2,132,2]{2,1,0:T(8,128)S(1)}, f32[2,132,2]{2,1,0:T(8,128)S(1)}, u32[]{:S(2)}, u32[]{:S(2)}) collective-permute-start(f32[2,132,2]{2,1,0:T(8,128)S(1)} %get-tuple-element.36), channel_id=1, source_target_pairs={{0,1},{1,2},{2,3},{3,4},{4,5},{5,6},{6,7},{7,0},{8,9},{9,10},{10,1... | collective-permute-start | bytes 6344 | tf_op jit(solution)/shard_map/ppermute | solution.py:30
  74.2 9.9 %collective-permute-start.22 = (f32[2,132,2]{2,1,0:T(8,128)S(1)}, f32[2,132,2]{2,1,0:T(8,128)S(1)}, u32[]{:S(2)}, u32[]{:S(2)}) collective-permute-start(f32[2,132,2]{2,1,0:T(8,128)S(1)} %get-tuple-element.37), channel_id=1, source_target_pairs={{1,0},{2,1},{3,2},{4,3},{5,4},{6,5},{7,6},{0,7},{9,8},{10,9},{11,1... | collective-permute-start | bytes 6344 | tf_op jit(solution)/shard_map/ppermute | solution.py:32
  88.6 8.9 %collective-permute-start.25 = (f32[2,132,2]{2,1,0:T(8,128)S(1)}, f32[2,132,2]{2,1,0:T(8,128)S(1)}, u32[]{:S(2)}, u32[]{:S(2)}) collective-permute-start(f32[2,132,2]{2,1,0:T(8,128)S(1)} %get-tuple-element.32), channel_id=1, source_target_pairs={{0,1},{1,2},{2,3},{3,4},{4,5},{5,6},{6,7},{7,0},{8,9},{9,10},{10,1... | collective-permute-start | bytes 6344 | tf_op jit(solution)/shard_map/ppermute | solution.py:30
  88.8 8.7 %collective-permute-start.26 = (f32[2,132,2]{2,1,0:T(8,128)S(1)}, f32[2,132,2]{2,1,0:T(8,128)S(1)}, u32[]{:S(2)}, u32[]{:S(2)}) collective-permute-start(f32[2,132,2]{2,1,0:T(8,128)S(1)} %get-tuple-element.33), channel_id=1, source_target_pairs={{1,0},{2,1},{3,2},{4,3},{5,4},{6,5},{7,6},{0,7},{9,8},{10,9},{11,1... | collective-permute-start | bytes 6344 | tf_op jit(solution)/shard_map/ppermute | solution.py:32
  102.2 8.7 %collective-permute-start.29 = (f32[2,132,2]{2,1,0:T(8,128)S(1)}, f32[2,132,2]{2,1,0:T(8,128)S(1)}, u32[]{:S(2)}, u32[]{:S(2)}) collective-permute-start(f32[2,132,2]{2,1,0:T(8,128)S(1)} %get-tuple-element.28), channel_id=1, source_target_pairs={{0,1},{1,2},{2,3},{3,4},{4,5},{5,6},{6,7},{7,0},{8,9},{9,10},{10,1... | collective-permute-start | bytes 6344 | tf_op jit(solution)/shard_map/ppermute | solution.py:30
  102.8 9.0 %collective-permute-start.30 = (f32[2,132,2]{2,1,0:T(8,128)S(1)}, f32[2,132,2]{2,1,0:T(8,128)S(1)}, u32[]{:S(2)}, u32[]{:S(2)}) collective-permute-start(f32[2,132,2]{2,1,0:T(8,128)S(1)} %get-tuple-element.29), channel_id=1, source_target_pairs={{1,0},{2,1},{3,2},{4,3},{5,4},{6,5},{7,6},{0,7},{9,8},{10,9},{11,1... | collective-permute-start | bytes 6344 | tf_op jit(solution)/shard_map/ppermute | solution.py:32
  116.5 8.6 %collective-permute-start.33 = (f32[2,132,2]{2,1,0:T(8,128)S(1)}, f32[2,132,2]{2,1,0:T(8,128)S(1)}, u32[]{:S(2)}, u32[]{:S(2)}) collective-permute-start(f32[2,132,2]{2,1,0:T(8,128)S(1)} %get-tuple-element.24), channel_id=1, source_target_pairs={{0,1},{1,2},{2,3},{3,4},{4,5},{5,6},{6,7},{7,0},{8,9},{9,10},{10,1... | collective-permute-start | bytes 6344 | tf_op jit(solution)/shard_map/ppermute | solution.py:30
  116.7 10.5 %collective-permute-start.34 = (f32[2,132,2]{2,1,0:T(8,128)S(1)}, f32[2,132,2]{2,1,0:T(8,128)S(1)}, u32[]{:S(2)}, u32[]{:S(2)}) collective-permute-start(f32[2,132,2]{2,1,0:T(8,128)S(1)} %get-tuple-element.25), channel_id=1, source_target_pairs={{1,0},{2,1},{3,2},{4,3},{5,4},{6,5},{7,6},{0,7},{9,8},{10,9},{11,1... | collective-permute-start | bytes 6344 | tf_op jit(solution)/shard_map/ppermute | solution.py:32
  131.9 9.0 %collective-permute-start.37 = (f32[2,132,2]{2,1,0:T(8,128)S(1)}, f32[2,132,2]{2,1,0:T(8,128)S(1)}, u32[]{:S(2)}, u32[]{:S(2)}) collective-permute-start(f32[2,132,2]{2,1,0:T(8,128)S(1)} %get-tuple-element.20), channel_id=1, source_target_pairs={{0,1},{1,2},{2,3},{3,4},{4,5},{5,6},{6,7},{7,0},{8,9},{9,10},{10,1... | collective-permute-start | bytes 6344 | tf_op jit(solution)/shard_map/ppermute | solution.py:30
  132.1 10.2 %collective-permute-start.38 = (f32[2,132,2]{2,1,0:T(8,128)S(1)}, f32[2,132,2]{2,1,0:T(8,128)S(1)}, u32[]{:S(2)}, u32[]{:S(2)}) collective-permute-start(f32[2,132,2]{2,1,0:T(8,128)S(1)} %get-tuple-element.21), channel_id=1, source_target_pairs={{1,0},{2,1},{3,2},{4,3},{5,4},{6,5},{7,6},{0,7},{9,8},{10,9},{11,1... | collective-permute-start | bytes 6344 | tf_op jit(solution)/shard_map/ppermute | solution.py:32
  (16 other events, 53.3 us)
